TPU v7x, 32 devices: a whole 2x2x4 slice. The times are simulated.
32 devices in a mesh: ctx: 2 (over y), row: 8 (over z, x), col: 2 (over core).
Axes of the slice: x: 2, y: 2, z: 4, core: 2. Of those that a mesh axis runs over, the one named last changes fastest.
Arguments:
- context_map: bfloat16 [128, 512, 256], P(('ctx', 'row'), 'col'), parts along dimension 0, may hold values from -6 to 6
- norm_gains: float32 [3, 256], replicated, may hold values from 0.25 to 1.75
- conv_biases: float32 [3, 256], replicated, may hold values from -3 to 3
- conv_weights: bfloat16 [3, 3, 3, 256, 256], replicated, may hold values from -0.125 to 0.125
Outputs:
- refined: bfloat16 [128, 512, 256], P(('ctx', 'row'), 'col'), parts along dimension 0
There are 2 independent parts, one for each index of `ctx`. A program takes and returns all parts, laid end to end along the dimension named above; an argument that names none is the same for every part. Nothing has to cross between parts.
All inputs are finite; a program needn't handle non-finite values.
Results may differ from a plain program's by a relative error of at most 0.0052.
Values may be sent and summed in bfloat16 or wider, within the bound.
A program may use at most 64 MiB of HBM per device.

v0:
```python
import jax
import jax.numpy as jnp
from jax import lax
from jax.sharding import PartitionSpec as P

epsilon = 1e-05


def extended(x, sides, width):
    for axis, dim in sides:
        size, length = (lax.axis_size(axis), x.shape[dim])
        up = [(i, (i + 1) % size) for i in range(size - 1)]
        down = [(j, i) for i, j in up]
        last = lax.slice_in_dim(x, length - width, length, axis=dim)
        first = lax.slice_in_dim(x, 0, width, axis=dim)
        before = lax.ppermute(last, axis, up)
        after = lax.ppermute(first, axis, down)
        x = jnp.concatenate([before, x, after], axis=dim)
    return x


def normalize(current, gain_row):
    values = current.astype(jnp.float32)
    centred = values - jnp.mean(values, axis=-1, keepdims=True)
    variance = jnp.mean(centred * centred, axis=-1, keepdims=True)
    return (centred * lax.rsqrt(variance + epsilon) * gain_row).astype(jnp.bfloat16)


def convolve(padded, kernel, row_step, col_step, out_rows, out_cols):
    channels = padded.shape[2]
    tap_list = []
    for tap_row in range(3):
        for tap_col in range(3):
            tap_list.append(
                lax.slice(
                    padded,
                    (tap_row * row_step, tap_col * col_step, 0),
                    (tap_row * row_step + out_rows, tap_col * col_step + out_cols, channels),
                )
            )
    stacked = jnp.concatenate(tap_list, axis=2).reshape(out_rows * out_cols, 9 * channels)
    product = jnp.dot(
        stacked, kernel.reshape(9 * channels, kernel.shape[3]), preferred_element_type=jnp.float32
    )
    return product.reshape(out_rows, out_cols, kernel.shape[3])


def update(current, response, bias_row):
    return (current.astype(jnp.float32) + jnp.maximum(response + bias_row, 0.0)).astype(
        jnp.bfloat16
    )


def class_rims(normed, width):
    return extended(normed, (("col", 1),), width)


def shards(context_map, norm_gains, conv_biases, conv_weights):
    tile_rows, tile_cols, channels = context_map.shape
    normed = normalize(context_map, norm_gains[0])
    padded = extended(normed, (("row", 0), ("col", 1)), 4)
    current = update(
        context_map, convolve(padded, conv_weights[0], 4, 4, tile_rows, tile_cols), conv_biases[0]
    )
    class_count = lax.axis_size("row") // tile_rows
    sub_cols = tile_cols // class_count
    outgoing = (
        current.reshape(tile_rows, sub_cols, class_count, channels)
        .transpose(0, 2, 1, 3)
        .reshape(tile_rows * class_count, sub_cols, channels)
    )
    grouped = lax.all_to_all(outgoing, "row", split_axis=0, concat_axis=0, tiled=True)
    sub_rows = grouped.shape[0]
    for position, dilation in ((1, 32), (2, 64)):
        normed = normalize(grouped, norm_gains[position])
        row_gap = dilation // tile_rows
        col_gap = dilation // class_count
        with_sides = class_rims(normed, col_gap)
        padded = jnp.pad(with_sides, ((row_gap, row_gap), (0, 0), (0, 0)))
        response = convolve(padded, conv_weights[position], row_gap, col_gap, sub_rows, sub_cols)
        grouped = update(grouped, response, conv_biases[position])
    returned = lax.all_to_all(grouped, "row", split_axis=0, concat_axis=0, tiled=True)
    return (
        returned.reshape(tile_rows, class_count, sub_cols, channels)
        .transpose(0, 2, 1, 3)
        .reshape(tile_rows, tile_cols, channels)
    )


def solution(mesh):
    return jax.shard_map(
        shards,
        mesh=mesh,
        in_specs=(P(("ctx", "row"), "col", None), P(), P(), P()),
        out_specs=P(("ctx", "row"), "col", None),
        check_vma=False,
    )
```

profile of v0, /device:TPU:0, one launch (start us, length us, event | category | flops | bytes accessed | tf_op | source)
XLA Modules:
  0.0 127.2 jit_solution(14104926304411926361)
XLA Ops:
  0.0 1.7 %convert_reduce_fusion.2 = f32[8,256]{1,0:T(8,128)S(1)} fusion(bf16[8,256,256]{2,1,0:T(8,128)(2,1)} %param.4), kind=kLoop, calls=%fused_computation.11 | loop fusion | flops 1046528 | bytes 1056768 | tf_op jit(solution)/shard_map/reduce_sum | solution.py:24
  1.7 1.9 %fusion.18 = f32[8,256]{1,0:T(8,128)S(1)} fusion(bf16[8,256,256]{2,1,0:T(8,128)(2,1)} %param.4, f32[8,256]{1,0:T(8,128)S(1)} %broadcast_multiply_fusion.2), kind=kLoop, calls=%fused_computation.31 | loop fusion | flops 2095104 | bytes 1064960 | tf_op jit(solution)/shard_map/reduce_sum | solution.py:25
  3.6 0.9 fusion.35
  4.5 0.7 fusion.20
  5.2 0.1 fusion.33
  5.3 4.9 %collective-permute-start = (bf16[4,256,256]{2,1,0:T(8,128)(2,1)S(1)}, bf16[4,256,256]{2,1,0:T(8,128)(2,1)S(1)}, u32[]{:S(2)}, u32[]{:S(2)}) collective-permute-start(bf16[4,256,256]{2,1,0:T(8,128)(2,1)S(1)} %get-tuple-element.16), channel_id=1, source_target_pairs={{0,2},{2,4},{4,6},{6,8},{8,10},{10,12},{12,14},{1,3},{3,5},{5,7},{... | collective-permute-start | bytes 1572872 | tf_op jit(solution)/shard_map/ppermute | solution.py:16
  10.2 1.3 %collective-permute-start.1 = (bf16[4,256,256]{2,1,0:T(8,128)(2,1)S(1)}, bf16[4,256,256]{2,1,0:T(8,128)(2,1)S(1)}, u32[]{:S(2)}, u32[]{:S(2)}) collective-permute-start(bf16[4,256,256]{2,1,0:T(8,128)(2,1)S(1)} %get-tuple-element.17), channel_id=1, source_target_pairs={{2,0},{4,2},{6,4},{8,6},{10,8},{12,10},{14,12},{3,1},{5,3},{7,5},{... | collective-permute-start | bytes 1572872 | tf_op jit(solution)/shard_map/ppermute | solution.py:17
  11.5 0.4 fusion.30
  11.9 20.7 %collective-permute-done = bf16[4,256,256]{2,1,0:T(8,128)(2,1)S(1)} collective-permute-done((bf16[4,256,256]{2,1,0:T(8,128)(2,1)S(1)}, bf16[4,256,256]{2,1,0:T(8,128)(2,1)S(1)}, u32[]{:S(2)}, u32[]{:S(2)}) %collective-permute-start) | collective-permute-done | bytes 524320 | tf_op jit(solution)/shard_map/ppermute | solution.py:16
  32.6 1.3 %collective-permute-start.2 = (bf16[16,4,256]{2,1,0:T(4,128)(2,1)S(1)}, bf16[16,4,256]{2,1,0:T(4,128)(2,1)S(1)}, u32[]{:S(2)}, u32[]{:S(2)}) collective-permute-start(bf16[16,4,256]{2,1,0:T(4,128)(2,1)S(1)} %get-tuple-element.11), channel_id=1, source_target_pairs={{0,1},{2,3},{4,5},{6,7},{8,9},{10,11},{12,13},{14,15},{16,17},{18,... | collective-permute-start | bytes 98312 | tf_op jit(solution)/shard_map/ppermute | solution.py:16
  33.9 1.3 %collective-permute-start.3 = (bf16[16,4,256]{2,1,0:T(4,128)(2,1)S(1)}, bf16[16,4,256]{2,1,0:T(4,128)(2,1)S(1)}, u32[]{:S(2)}, u32[]{:S(2)}) collective-permute-start(bf16[16,4,256]{2,1,0:T(4,128)(2,1)S(1)} %get-tuple-element.10), channel_id=1, source_target_pairs={{1,0},{3,2},{5,4},{7,6},{9,8},{11,10},{13,12},{15,14},{17,16},{19,... | collective-permute-start | bytes 98312 | tf_op jit(solution)/shard_map/ppermute | solution.py:17
  35.2 1.8 %collective-permute-done.3 = bf16[16,4,256]{2,1,0:T(4,128)(2,1)S(1)} collective-permute-done((bf16[16,4,256]{2,1,0:T(4,128)(2,1)S(1)}, bf16[16,4,256]{2,1,0:T(4,128)(2,1)S(1)}, u32[]{:S(2)}, u32[]{:S(2)}) %collective-permute-start.3) | collective-permute-done | bytes 32800 | tf_op jit(solution)/shard_map/ppermute | solution.py:17
  37.0 1.0 pad_maximum_fusion
  38.0 0.1 fusion.29
  38.1 0.2 slice_dynamic-update-slice_fusion.10
  38.4 0.1 slice_dynamic-update-slice_fusion.9
  38.5 0.7 constant_dynamic-update-slice_fusion
  39.2 0.2 slice_dynamic-update-slice_fusion.8
  39.4 0.1 slice_dynamic-update-slice_fusion.7
  39.5 0.1 fusion.28
  39.6 0.2 slice_dynamic-update-slice_fusion.6
  39.9 2.6 %fusion.21 = bf16[8,256,256]{2,1,0:T(8,128)(2,1)S(1)} fusion(bf16[8,256,256]{2,1,0:T(8,128)(2,1)S(1)} %copy-done, bf16[8,256,2304]{2,1,0:T(8,128)(2,1)S(1)} %slice_dynamic-update-slice_fusion.6, bf16[2304,256,1]{1,0,2:T(8,128)(2,1)S(1)} %bitcast.23, f32[256]{0:T(256)S(1)} %bitcast.32), kind=kOutput, calls=%fused_computation.34 | convolution fusion | flops 2418540544 | bytes 12715008 | tf_op jit(solution)/shard_map/dot_general | solution.py:42
  42.5 33.2 %all_to_all.10 = bf16[8,256,256]{2,1,0:T(8,128)(2,1)S(1)} all-to-all(bf16[8,256,256]{2,1,0:T(8,128)(2,1)S(1)} %fusion.21), channel_id=1, replica_groups=mesh['ctx'=2,'row'=8,'col'=2] {'row'}, dimensions={0} | all-to-all | bytes 2097152 | tf_op jit(solution)/shard_map/all_to_all | solution.py:72
  75.8 0.3 convert_reduce_fusion.1
  76.1 0.6 fusion.15
  76.8 0.7 fusion.17
  77.5 1.3 %collective-permute-start.4 = (bf16[8,32,256]{2,1,0:T(8,128)(2,1)S(1)}, bf16[8,32,256]{2,1,0:T(8,128)(2,1)S(1)}, u32[]{:S(2)}, u32[]{:S(2)}) collective-permute-start(bf16[8,32,256]{2,1,0:T(8,128)(2,1)S(1)} %get-tuple-element.14), channel_id=1, source_target_pairs={{0,1},{2,3},{4,5},{6,7},{8,9},{10,11},{12,13},{14,15},{16,17},{18,... | collective-permute-start | bytes 393224 | tf_op jit(solution)/shard_map/ppermute | solution.py:16
  78.8 1.5 %collective-permute-start.5 = (bf16[8,32,256]{2,1,0:T(8,128)(2,1)S(1)}, bf16[8,32,256]{2,1,0:T(8,128)(2,1)S(1)}, u32[]{:S(2)}, u32[]{:S(2)}) collective-permute-start(bf16[8,32,256]{2,1,0:T(8,128)(2,1)S(1)} %get-tuple-element.15), channel_id=1, source_target_pairs={{1,0},{3,2},{5,4},{7,6},{9,8},{11,10},{13,12},{15,14},{17,16},{19,... | collective-permute-start | bytes 393224 | tf_op jit(solution)/shard_map/ppermute | solution.py:17
  80.4 1.7 %collective-permute-done.5 = bf16[8,32,256]{2,1,0:T(8,128)(2,1)S(1)} collective-permute-done((bf16[8,32,256]{2,1,0:T(8,128)(2,1)S(1)}, bf16[8,32,256]{2,1,0:T(8,128)(2,1)S(1)}, u32[]{:S(2)}, u32[]{:S(2)}) %collective-permute-start.5) | collective-permute-done | bytes 131104 | tf_op jit(solution)/shard_map/ppermute | solution.py:17
  82.1 0.4 fusion.5
  82.6 0.1 slice_dynamic-update-slice_fusion.4
  82.7 0.1 slice_dynamic-update-slice_fusion.3
  82.7 0.1 fusion.27
  82.8 0.7 constant_dynamic-update-slice_fusion.1
  83.5 0.1 fusion.26
  83.6 0.1 slice_dynamic-update-slice_fusion.2
  83.7 0.1 slice_dynamic-update-slice_fusion.1
  83.9 2.7 %convert_reduce_fusion = (f32[8,256]{1,0:T(8,128)S(1)}, bf16[8,256,256]{2,1,0:T(8,128)(2,1)S(1)}) fusion(f32[256]{0:T(256)S(1)} %bitcast.31, bf16[8,256,2304]{2,1,0:T(8,128)(2,1)S(1)} %slice_dynamic-update-slice_fusion, bf16[2304,256,1]{1,0,2:T(8,128)(2,1)S(1)} %bitcast.22, bf16[8,256,256]{2,1,0:T(8,128)(2,1)S(1)} %all_to_all.10), kind=kOutput, calls=%fused_computation.5 | convolution fusion | flops 2419587072 | bytes 12723200 | tf_op jit(solution)/shard_map/dot_general | solution.py:42
  86.6 0.6 fusion.12
  87.3 0.7 fusion.14
  88.0 2.1 %collective-permute-start.6 = (bf16[8,64,256]{2,1,0:T(8,128)(2,1)S(1)}, bf16[8,64,256]{2,1,0:T(8,128)(2,1)S(1)}, u32[]{:S(2)}, u32[]{:S(2)}) collective-permute-start(bf16[8,64,256]{2,1,0:T(8,128)(2,1)S(1)} %get-tuple-element.13), channel_id=1, source_target_pairs={{0,1},{2,3},{4,5},{6,7},{8,9},{10,11},{12,13},{14,15},{16,17},{18,... | collective-permute-start | bytes 786440 | tf_op jit(solution)/shard_map/ppermute | solution.py:16
  90.3 1.3 %collective-permute-start.7 = (bf16[8,64,256]{2,1,0:T(8,128)(2,1)S(1)}, bf16[8,64,256]{2,1,0:T(8,128)(2,1)S(1)}, u32[]{:S(2)}, u32[]{:S(2)}) collective-permute-start(bf16[8,64,256]{2,1,0:T(8,128)(2,1)S(1)} %get-tuple-element.12), channel_id=1, source_target_pairs={{1,0},{3,2},{5,4},{7,6},{9,8},{11,10},{13,12},{15,14},{17,16},{19,... | collective-permute-start | bytes 786440 | tf_op jit(solution)/shard_map/ppermute | solution.py:17
  91.6 0.1 fusion.25
  91.7 0.7 constant_dynamic-update-slice_fusion.2
  92.4 1.3 %collective-permute-done.7 = bf16[8,64,256]{2,1,0:T(8,128)(2,1)S(1)} collective-permute-done((bf16[8,64,256]{2,1,0:T(8,128)(2,1)S(1)}, bf16[8,64,256]{2,1,0:T(8,128)(2,1)S(1)}, u32[]{:S(2)}, u32[]{:S(2)}) %collective-permute-start.7) | collective-permute-done | bytes 262176 | tf_op jit(solution)/shard_map/ppermute | solution.py:17
  94.0 2.6 %fusion.23 = bf16[8,256,256]{2,1,0:T(8,128)(2,1)S(1)} fusion(bf16[8,256,256]{2,1,0:T(8,128)(2,1)S(1)} %get-tuple-element.25, bf16[8,256,2304]{2,1,0:T(8,128)(2,1)S(1)} %broadcast_dynamic-update-slice_fusion.5, bf16[2304,256,1]{1,0,2:T(8,128)(2,1)S(1)} %bitcast.21, f32[256]{0:T(256)S(1)} %bitcast.30), kind=kOutput, calls=%fused_computation.36 | convolution fusion | flops 2418540544 | bytes 12715008 | tf_op jit(solution)/shard_map/dot_general | solution.py:42
  96.7 29.6 %all_to_all.11 = bf16[8,256,256]{2,1,0:T(8,128)(2,1)S(1)} all-to-all(bf16[8,256,256]{2,1,0:T(8,128)(2,1)S(1)} %fusion.23), channel_id=1, replica_groups=mesh['ctx'=2,'row'=8,'col'=2] {'row'}, dimensions={0} | all-to-all | bytes 2097152 | tf_op jit(solution)/shard_map/all_to_all | solution.py:82
  126.2 1.0 copy.30
  (30 shorter events, 0.9 us)
Async XLA Ops:
  0.0 4.5 %copy-start = (bf16[8,256,256]{2,1,0:T(8,128)(2,1)S(1)}, bf16[8,256,256]{2,1,0:T(8,128)(2,1)}, u32[]{:S(2)}) copy-start(bf16[8,256,256]{2,1,0:T(8,128)(2,1)} %param.4) | copy-start | bytes 3145732
  3.6 7.9 %copy-start.1 = (bf16[3,3,3,256,256]{4,3,2,1,0:T(8,128)(2,1)S(1)}, bf16[3,3,3,256,256]{4,3,2,1,0:T(8,128)(2,1)}, u32[]{:S(2)}) copy-start(bf16[3,3,3,256,256]{4,3,2,1,0:T(8,128)(2,1)} %param.7) | copy-start | bytes 10616836
  5.3 27.3 %collective-permute-start = (bf16[4,256,256]{2,1,0:T(8,128)(2,1)S(1)}, bf16[4,256,256]{2,1,0:T(8,128)(2,1)S(1)}, u32[]{:S(2)}, u32[]{:S(2)}) collective-permute-start(bf16[4,256,256]{2,1,0:T(8,128)(2,1)S(1)} %get-tuple-element.16), channel_id=1, source_target_pairs={{0,2},{2,4},{4,6},{6,8},{8,10},{10,12},{12,14},{1,3},{3,5},{5,7},{... | collective-permute-start | bytes 1572872 | tf_op jit(solution)/shard_map/ppermute | solution.py:16
  10.2 22.4 %collective-permute-start.1 = (bf16[4,256,256]{2,1,0:T(8,128)(2,1)S(1)}, bf16[4,256,256]{2,1,0:T(8,128)(2,1)S(1)}, u32[]{:S(2)}, u32[]{:S(2)}) collective-permute-start(bf16[4,256,256]{2,1,0:T(8,128)(2,1)S(1)} %get-tuple-element.17), channel_id=1, source_target_pairs={{2,0},{4,2},{6,4},{8,6},{10,8},{12,10},{14,12},{3,1},{5,3},{7,5},{... | collective-permute-start | bytes 1572872 | tf_op jit(solution)/shard_map/ppermute | solution.py:17
  11.9 23.3 %copy-start.2 = (f32[3,256]{1,0:T(4,128)S(1)}, f32[3,256]{1,0:T(4,128)}, u32[]{:S(2)}) copy-start(f32[3,256]{1,0:T(4,128)} %param.6) | copy-start | bytes 9220
  32.6 2.6 %collective-permute-start.2 = (bf16[16,4,256]{2,1,0:T(4,128)(2,1)S(1)}, bf16[16,4,256]{2,1,0:T(4,128)(2,1)S(1)}, u32[]{:S(2)}, u32[]{:S(2)}) collective-permute-start(bf16[16,4,256]{2,1,0:T(4,128)(2,1)S(1)} %get-tuple-element.11), channel_id=1, source_target_pairs={{0,1},{2,3},{4,5},{6,7},{8,9},{10,11},{12,13},{14,15},{16,17},{18,... | collective-permute-start | bytes 98312 | tf_op jit(solution)/shard_map/ppermute | solution.py:16
  33.9 3.1 %collective-permute-start.3 = (bf16[16,4,256]{2,1,0:T(4,128)(2,1)S(1)}, bf16[16,4,256]{2,1,0:T(4,128)(2,1)S(1)}, u32[]{:S(2)}, u32[]{:S(2)}) collective-permute-start(bf16[16,4,256]{2,1,0:T(4,128)(2,1)S(1)} %get-tuple-element.10), channel_id=1, source_target_pairs={{1,0},{3,2},{5,4},{7,6},{9,8},{11,10},{13,12},{15,14},{17,16},{19,... | collective-permute-start | bytes 98312 | tf_op jit(solution)/shard_map/ppermute | solution.py:17
  77.5 2.9 %collective-permute-start.4 = (bf16[8,32,256]{2,1,0:T(8,128)(2,1)S(1)}, bf16[8,32,256]{2,1,0:T(8,128)(2,1)S(1)}, u32[]{:S(2)}, u32[]{:S(2)}) collective-permute-start(bf16[8,32,256]{2,1,0:T(8,128)(2,1)S(1)} %get-tuple-element.14), channel_id=1, source_target_pairs={{0,1},{2,3},{4,5},{6,7},{8,9},{10,11},{12,13},{14,15},{16,17},{18,... | collective-permute-start | bytes 393224 | tf_op jit(solution)/shard_map/ppermute | solution.py:16
  78.8 3.2 %collective-permute-start.5 = (bf16[8,32,256]{2,1,0:T(8,128)(2,1)S(1)}, bf16[8,32,256]{2,1,0:T(8,128)(2,1)S(1)}, u32[]{:S(2)}, u32[]{:S(2)}) collective-permute-start(bf16[8,32,256]{2,1,0:T(8,128)(2,1)S(1)} %get-tuple-element.15), channel_id=1, source_target_pairs={{1,0},{3,2},{5,4},{7,6},{9,8},{11,10},{13,12},{15,14},{17,16},{19,... | collective-permute-start | bytes 393224 | tf_op jit(solution)/shard_map/ppermute | solution.py:17
  88.0 3.5 %collective-permute-start.6 = (bf16[8,64,256]{2,1,0:T(8,128)(2,1)S(1)}, bf16[8,64,256]{2,1,0:T(8,128)(2,1)S(1)}, u32[]{:S(2)}, u32[]{:S(2)}) collective-permute-start(bf16[8,64,256]{2,1,0:T(8,128)(2,1)S(1)} %get-tuple-element.13), channel_id=1, source_target_pairs={{0,1},{2,3},{4,5},{6,7},{8,9},{10,11},{12,13},{14,15},{16,17},{18,... | collective-permute-start | bytes 786440 | tf_op jit(solution)/shard_map/ppermute | solution.py:16
  90.3 3.4 %collective-permute-start.7 = (bf16[8,64,256]{2,1,0:T(8,128)(2,1)S(1)}, bf16[8,64,256]{2,1,0:T(8,128)(2,1)S(1)}, u32[]{:S(2)}, u32[]{:S(2)}) collective-permute-start(bf16[8,64,256]{2,1,0:T(8,128)(2,1)S(1)} %get-tuple-element.12), channel_id=1, source_target_pairs={{1,0},{3,2},{5,4},{7,6},{9,8},{11,10},{13,12},{15,14},{17,16},{19,... | collective-permute-start | bytes 786440 | tf_op jit(solution)/shard_map/ppermute | solution.py:17
where the time goes:
time: 128 us; the launch traced here: 127 us
  blocking collectives  62.8 us (49%)
  waiting for transfers between devices  25.4 us (20%)
  starting transfers between devices  14.9 us (12%)
  other arithmetic  11.4 us (9%)
  matrix products  8.02 us (6%)
  local copies, waits for them, and re-layouts  4.17 us (3%)
    all_to_all x1, blocking collectives, shards(): lax.all_to_all(outgoing, 'row', split_axis=0, concat_axis=0, tiled=True)  33.2 us
    all_to_all x1, blocking collectives, shards(): lax.all_to_all(grouped, 'row', split_axis=0, concat_axis=0, tiled=True)  29.6 us
    ppermute x4, waiting for transfers between devices, extended(): before = lax.ppermute(last, axis, up)  20.7 us
    ppermute x4, starting transfers between devices, extended(): before = lax.ppermute(last, axis, up)  9.56 us
    dot_general x3, matrix products, convolve(): jnp.dot(stacked, kernel.reshape(9 * channels, kernel.shape[3]), preferred...  8.02 us
    ppermute x4, starting transfers between devices, extended(): after = lax.ppermute(first, axis, down)  5.35 us
    ppermute x4, waiting for transfers between devices, extended(): after = lax.ppermute(first, axis, down)  4.76 us
    reduce_sum x3, other arithmetic, normalize(): variance = jnp.mean(centred * centred, axis=-1, keepdims=True)  3.16 us
  transfers between devices with their start and end apart: 8, of which 4 were waited for; matrix products, arithmetic and copies ran while one was open for 1% of the time, Pallas kernels for 0%

commit v1 on v0

--- a/solution.py
+++ b/solution.py
@@ -1,9 +1,14 @@
+import functools
+
 import jax
 import jax.numpy as jnp
 from jax import lax
+from jax.experimental import pallas as pl
+from jax.experimental.pallas import tpu as pltpu
 from jax.sharding import PartitionSpec as P
 
 epsilon = 1e-05
+dilations = (4, 32, 64)
 
 
 def extended(x, sides, width):
@@ -55,6 +60,390 @@
     return extended(normed, (("col", 1),), width)
 
 
+def streamed(
+    x_hbm, g_ref, b_ref, w_hbm, out_hbm,
+    xs, n0, taps, n1, m1, n2, x1, x2, y, w,
+    load_sem, w_sem, dn_send, dn_recv, up_send, up_recv, side_send, side_recv,
+    swap_send, swap_recv, rim_send, rim_recv, out_sem,
+):
+    tile_rows, tile_cols, channels = x_hbm.shape
+    halo, wide = dilations[0], dilations[1]
+    edge = 16
+    slots = tile_cols // wide
+    cells = tile_rows * wide
+    i, n = lax.axis_index("row"), lax.axis_size("row")
+    c = lax.axis_index("col")
+    other = 1 - c
+    above, below = lax.rem(i + n - 1, n), lax.rem(i + 1, n)
+    shift = dilations[1] // tile_rows
+    partner = lax.rem(i + shift, n)
+    partner_tap = jnp.where(i < shift, 2, 0)
+    outward = 1 - 2 * c
+    has_above, has_below = i > 0, i < n - 1
+
+    def columns(s):
+        return pl.ds(
+            pl.multiple_of(c * wide * (s - 1) + other * (tile_cols - wide * s), wide), wide
+        )
+
+    def remote(src, dst, send, recv, row, col):
+        return pltpu.make_async_remote_copy(
+            src_ref=src,
+            dst_ref=dst,
+            send_sem=send,
+            recv_sem=recv,
+            device_id={"row": row, "col": col},
+            device_id_type=pl.DeviceIdType.MESH,
+        )
+
+    def load(s):
+        return pltpu.make_async_copy(
+            x_hbm.at[:, columns(s), :], xs.at[s, halo : halo + tile_rows], load_sem.at[s - 1]
+        )
+
+    def load_w(layer):
+        return pltpu.make_async_copy(w_hbm.at[layer], w.at[layer], w_sem.at[layer])
+
+    def halo_down(s):
+        return remote(
+            x_hbm.at[tile_rows - halo :, columns(s), :], xs.at[s, :halo],
+            dn_send.at[s - 1], dn_recv.at[s - 1], below, c,
+        )
+
+    def halo_up(s):
+        return remote(
+            x_hbm.at[:halo, columns(s), :], xs.at[s, halo + tile_rows :],
+            up_send.at[s - 1], up_recv.at[s - 1], above, c,
+        )
+
+    side_from = pl.ds(pl.multiple_of(other * (tile_cols - edge), edge), edge)
+    side_to = pl.ds(pl.multiple_of(other * (wide - edge), edge), edge)
+
+    side = remote(
+        x_hbm.at[:, side_from, :], xs.at[0, halo : halo + tile_rows, side_to, :],
+        side_send.at[0], side_recv.at[0], i, other,
+    )
+    corner_down = remote(
+        x_hbm.at[tile_rows - halo :, side_from, :], xs.at[0, :halo, side_to, :],
+        side_send.at[1], side_recv.at[1], below, other,
+    )
+    corner_up = remote(
+        x_hbm.at[:halo, side_from, :], xs.at[0, halo + tile_rows :, side_to, :],
+        side_send.at[2], side_recv.at[2], above, other,
+    )
+
+    def swap(s):
+        return remote(
+            n1.at[s], m1.at[s], swap_send.at[s - 1], swap_recv.at[s - 1], partner, c
+        )
+
+    rim_own = remote(n1.at[1], n1.at[0], rim_send.at[0], rim_recv.at[0], i, other)
+    rim_partner = remote(m1.at[1], m1.at[0], rim_send.at[1], rim_recv.at[1], i, other)
+    rim_next = [
+        remote(n2.at[1 + s], n2.at[2 - s], rim_send.at[1 + s], rim_recv.at[1 + s], i, other)
+        for s in (1, 2)
+    ]
+
+    def store(s):
+        return pltpu.make_async_copy(
+            y.at[s - 1], out_hbm.at[:, columns(s), :], out_sem.at[s - 1]
+        )
+
+    def norm(values, layer):
+        values = values.astype(jnp.float32)
+        centred = values - jnp.mean(values, axis=-1, keepdims=True)
+        variance = jnp.mean(centred * centred, axis=-1, keepdims=True)
+        gain = g_ref[layer : layer + 1, :].reshape((1,) * (values.ndim - 1) + (channels,))
+        return (centred * lax.rsqrt(variance + epsilon) * gain).astype(jnp.bfloat16)
+
+    def residual(values, response, layer):
+        return (
+            values.reshape(cells, channels).astype(jnp.float32)
+            + jnp.maximum(response + b_ref[layer : layer + 1, :], 0.0)
+        ).astype(jnp.bfloat16)
+
+    def dot(a, b):
+        return jnp.dot(a, b, preferred_element_type=jnp.float32)
+
+    def row_of(ref, s, step):
+        return jnp.concatenate(
+            [ref[at].reshape(cells, channels) for at in (s + step, s, s - step)], axis=1
+        )
+
+    @pl.loop(1, slots + 1)
+    def _(s):
+        load(s).start()
+
+    for layer in range(3):
+        load_w(layer).start()
+
+    barrier = pltpu.get_barrier_semaphore()
+    zeros = functools.partial(jnp.zeros, dtype=jnp.bfloat16)
+    xs[0] = zeros(xs.shape[1:])
+
+    @pl.when(i == 0)
+    def _():
+        xs[:, :halo] = zeros((slots + 1, halo, wide, channels))
+
+    @pl.when(i == n - 1)
+    def _():
+        xs[:, halo + tile_rows :] = zeros((slots + 1, halo, wide, channels))
+
+    def greet(row, col):
+        pl.semaphore_signal(
+            barrier, inc=1, device_id={"row": row, "col": col},
+            device_id_type=pl.DeviceIdType.MESH,
+        )
+
+    greet(i, other)
+    greet(partner, c)
+
+    @pl.when(has_above)
+    def _():
+        greet(above, c)
+        greet(above, other)
+
+    @pl.when(has_below)
+    def _():
+        greet(below, c)
+        greet(below, other)
+
+    n0[slots + 1] = zeros(n0.shape[1:])
+    n1[slots + 1] = zeros(n1.shape[1:])
+    m1[slots + 1] = zeros(m1.shape[1:])
+    n2[slots + 2] = zeros(n2.shape[1:])
+    n2[slots + 3] = zeros(n2.shape[1:])
+    pl.semaphore_wait(barrier, 2 + 2 * jnp.minimum(i, 1) + 2 * jnp.minimum(n - 1 - i, 1))
+
+    side.start()
+
+    @pl.when(has_below)
+    def _():
+        corner_down.start()
+
+    @pl.when(has_above)
+    def _():
+        corner_up.start()
+
+    @pl.loop(1, slots + 1)
+    def _(s):
+        @pl.when(has_below)
+        def _():
+            halo_down(s).start()
+
+        @pl.when(has_above)
+        def _():
+            halo_up(s).start()
+
+    def arrive(s):
+        load(s).wait()
+
+        @pl.when(has_above)
+        def _():
+            halo_down(s).wait_recv()
+
+        @pl.when(has_below)
+        def _():
+            halo_up(s).wait_recv()
+
+    def norm_slot(s):
+        @pl.loop(0, xs.shape[1] // halo)
+        def _(part):
+            rows = pl.ds(part * halo, halo)
+            n0[s, rows] = norm(xs[s, rows], 0)
+
+    side.wait_recv()
+
+    @pl.when(has_above)
+    def _():
+        corner_down.wait_recv()
+
+    @pl.when(has_below)
+    def _():
+        corner_up.wait_recv()
+
+    load_w(0).wait()
+
+    @pl.loop(0, slots + 2)
+    def _(s):
+        @pl.when((s > 0) & (s <= slots))
+        def _():
+            arrive(s)
+
+        @pl.when(s <= slots)
+        def _():
+            norm_slot(s)
+
+        @pl.when(s > 1)
+        def _():
+            at = s - 1
+            left, right = at + outward, at - outward
+
+            @pl.loop(0, xs.shape[1] // halo)
+            def _(part):
+                rows = pl.ds(part * halo, halo)
+                centre = n0[at, rows]
+                around = jnp.concatenate(
+                    [n0[left, rows, wide - edge :, :], centre, n0[right, rows, :edge, :]], axis=1
+                ).astype(jnp.float32)
+                span = wide + 2 * edge
+                lower = pltpu.roll(around, halo, 1)[:, edge : edge + wide]
+                upper = pltpu.roll(around, span - halo, 1)[:, edge : edge + wide]
+                taps[rows, :, :channels] = lower.astype(jnp.bfloat16)
+                taps[rows, :, channels : 2 * channels] = centre
+                taps[rows, :, 2 * channels :] = upper.astype(jnp.bfloat16)
+
+            response = dot(taps[:tile_rows].reshape(cells, 3 * channels), w[0, 0])
+            for tap in (1, 2):
+                response += dot(
+                    taps[tap * halo : tap * halo + tile_rows].reshape(cells, 3 * channels),
+                    w[0, tap],
+                )
+            current = residual(xs[at, halo : halo + tile_rows], response, 0)
+            x1[at - 1] = current
+            n1[at] = norm(current, 1).reshape(tile_rows, wide, channels)
+            swap(at).start()
+
+            @pl.when(at == 1)
+            def _():
+                rim_own.start()
+
+    load_w(1).wait()
+    load_w(2).wait()
+    rim_own.wait_recv()
+    swap(1).wait_recv()
+    rim_partner.start()
+
+    @pl.loop(1, slots + 3)
+    def _(s):
+        @pl.when(s < slots)
+        def _():
+            swap(s + 1).wait_recv()
+
+        @pl.when(s == 1)
+        def _():
+            rim_partner.wait_recv()
+
+        @pl.when(s <= slots)
+        def _():
+            response = dot(row_of(n1, s, outward), w[1, 1])
+            response += dot(row_of(m1, s, outward), w[1, partner_tap])
+            current = residual(x1[s - 1].reshape(tile_rows, wide, channels), response, 1)
+            x2[s - 1] = current
+            n2[s + 1] = norm(current, 2).reshape(tile_rows, wide, channels)
+
+        for k in (1, 2):
+            @pl.when(s == k)
+            def _():
+                rim_next[k - 1].start()
+
+        @pl.when(s == 3)
+        def _():
+            for copy in rim_next:
+                copy.wait_recv()
+
+        @pl.when(s >= 3)
+        def _():
+            at = s - 2
+            response = dot(row_of(n2, at + 1, 2 * outward), w[2, 1])
+            current = residual(x2[at - 1].reshape(tile_rows, wide, channels), response, 2)
+            y[at - 1] = current.reshape(tile_rows, wide, channels)
+            store(at).start()
+
+    side.wait_send()
+    rim_own.wait_send()
+    rim_partner.wait_send()
+    for copy in rim_next:
+        copy.wait_send()
+
+    @pl.when(has_below)
+    def _():
+        corner_down.wait_send()
+
+    @pl.when(has_above)
+    def _():
+        corner_up.wait_send()
+
+    @pl.loop(1, slots + 1)
+    def _(s):
+        @pl.when(has_below)
+        def _():
+            halo_down(s).wait_send()
+
+        @pl.when(has_above)
+        def _():
+            halo_up(s).wait_send()
+
+        swap(s).wait_send()
+        store(s).wait()
+
+
+def paired(mesh, shape):
+    tile_rows, tile_cols, channels = shape
+    rows = mesh["row"] * tile_rows
+    return (
+        mesh["col"] == 2
+        and rows == 2 * dilations[1]
+        and rows <= dilations[2]
+        and dilations[2] == 2 * dilations[1]
+        and dilations[1] % tile_rows == 0
+        and mesh["row"] > 2
+        and tile_rows == 2 * dilations[0]
+        and tile_cols % dilations[1] == 0
+        and tile_cols >= dilations[2]
+        and channels % 128 == 0
+    )
+
+
+def streamed_shards(context_map, norm_gains, conv_biases, conv_weights):
+    tile_rows, tile_cols, channels = context_map.shape
+    halo, wide = dilations[0], dilations[1]
+    slots = tile_cols // wide
+    tall = tile_rows + 2 * halo
+    bf16 = jnp.bfloat16
+    dma = pltpu.SemaphoreType.DMA
+    cell = (tile_rows, wide, channels)
+    return pl.pallas_call(
+        streamed,
+        out_shape=jax.ShapeDtypeStruct(context_map.shape, bf16),
+        in_specs=[
+            pl.BlockSpec(memory_space=pltpu.HBM),
+            pl.BlockSpec(memory_space=pltpu.VMEM),
+            pl.BlockSpec(memory_space=pltpu.VMEM),
+            pl.BlockSpec(memory_space=pltpu.HBM),
+        ],
+        out_specs=pl.BlockSpec(memory_space=pltpu.HBM),
+        scratch_shapes=[
+            pltpu.VMEM((slots + 1, tall, wide, channels), bf16),
+            pltpu.VMEM((slots + 2, tall, wide, channels), bf16),
+            pltpu.VMEM((tall, wide, 3 * channels), bf16),
+            pltpu.VMEM((slots + 2,) + cell, bf16),
+            pltpu.VMEM((slots + 2,) + cell, bf16),
+            pltpu.VMEM((slots + 4,) + cell, bf16),
+            pltpu.VMEM((slots, tile_rows * wide, channels), bf16),
+            pltpu.VMEM((slots, tile_rows * wide, channels), bf16),
+            pltpu.VMEM((slots,) + cell, bf16),
+            pltpu.VMEM((3, 3, 3 * channels, channels), bf16),
+            dma((slots,)),
+            dma((3,)),
+            dma((slots,)), dma((slots,)),
+            dma((slots,)), dma((slots,)),
+            dma((3,)), dma((3,)),
+            dma((slots,)), dma((slots,)),
+            dma((4,)), dma((4,)),
+            dma((slots,)),
+        ],
+        compiler_params=pltpu.CompilerParams(
+            collective_id=0, has_side_effects=True, vmem_limit_bytes=48 * 1024 * 1024
+        ),
+    )(
+        context_map,
+        norm_gains,
+        conv_biases,
+        conv_weights.reshape(3, 3, 3 * channels, channels),
+    )
+
+
 def shards(context_map, norm_gains, conv_biases, conv_weights):
     tile_rows, tile_cols, channels = context_map.shape
     normed = normalize(context_map, norm_gains[0])
@@ -87,9 +476,14 @@
     )
 
 
+def by_shape(sizes, context_map, *parameters):
+    body = streamed_shards if paired(sizes, context_map.shape) else shards
+    return body(context_map, *parameters)
+
+
 def solution(mesh):
     return jax.shard_map(
-        shards,
+        functools.partial(by_shape, dict(mesh.shape)),
         mesh=mesh,
         in_specs=(P(("ctx", "row"), "col", None), P(), P(), P()),
         out_specs=P(("ctx", "row"), "col", None),

time: 128 us -> 80.4 us (0.63)
  Pallas kernels: 0 us -> 74.6 us
  blocking collectives: 62.8 us -> 0 us
  waiting for transfers between devices: 25.4 us -> 0 us
  starting transfers between devices: 14.9 us -> 0 us
  other arithmetic: 11.4 us -> 0 us
  matrix products: 8.02 us -> 0 us
  local copies, waits for them, and re-layouts: 4.17 us -> 5.57 us
    pallas_call x0 -> x1, Pallas kernels: none -> 74.6 us  [streamed_shards(): pl.pallas_call(streamed, out_shape=jax.ShapeDtypeStruct(context_map.shape...]
    all_to_all x2 -> x0, blocking collectives: 62.8 us -> none  [the longest x1 33.2 us: shards(): lax.all_to_all(outgoing, 'row', split_axis=0, concat_axis=0, tiled=True)]
    ppermute x8 -> x0, waiting for transfers between devices: 25.4 us -> none  [the longest x4 20.7 us: extended(): before = lax.ppermute(last, axis, up)]
    ppermute x8 -> x0, starting transfers between devices: 14.9 us -> none  [the longest x4 9.56 us: extended(): before = lax.ppermute(last, axis, up)]
    dot_general x3 -> x0, matrix products: 8.02 us -> none  [convolve(): jnp.dot(stacked, kernel.reshape(9 * channels, kernel.shape[3]), preferred...]
    reduce_sum x5 -> x0, other arithmetic: 5.16 us -> none  [the longest x3 3.16 us: normalize(): variance = jnp.mean(centred * centred, axis=-1, keepdims=True)]
    unnamed x22 -> x9, local copies, waits for them, and re-layouts: 2.39 us -> 5.57 us
    unnamed x9 -> x0, other arithmetic: 2.59 us -> none
  transfers between devices with their start and end apart: 8 -> 0, of which waited for: 4 -> 0; matrix products, arithmetic and copies ran while one was open for 1% -> 0% of each run, Pallas kernels for 0% -> 0%
where the time goes in v1:
time: 80.4 us; the launch traced here: 80.2 us
  Pallas kernels  74.6 us (93%)
  local copies, waits for them, and re-layouts  5.57 us (7%)
    pallas_call x1, Pallas kernels, streamed_shards(): pl.pallas_call(streamed, out_shape=jax.ShapeDtypeStruct(context_map.shape...  74.6 us
    unnamed x9, local copies, waits for them, and re-layouts  5.57 us

profile of v1, /device:TPU:0, one launch (start us, length us, event | category | flops | bytes accessed | tf_op | source)
XLA Modules:
  0.0 80.2 jit_solution(3933094887147752500)
XLA Ops:
  0.0 0.0 copy-start
  0.0 2.0 %copy-done = bf16[3,3,3,256,256]{4,3,2,1,0:T(8,128)(2,1)S(1)} copy-done((bf16[3,3,3,256,256]{4,3,2,1,0:T(8,128)(2,1)S(1)}, bf16[3,3,3,256,256]{4,3,2,1,0:T(8,128)(2,1)}, u32[]{:S(2)}) %copy-start) | copy-done | bytes 3538968
  2.0 0.0 copy-start.1
  2.0 1.2 %copy-done.1 = bf16[8,256,256]{2,1,0:T(8,128)(2,1)S(1)} copy-done((bf16[8,256,256]{2,1,0:T(8,128)(2,1)S(1)}, bf16[8,256,256]{2,1,0:T(8,128)(2,1)}, u32[]{:S(2)}) %copy-start.1) | copy-done | bytes 1048600
  3.2 0.0 copy-start.2
  3.2 0.7 copy-done.2
  3.9 0.0 copy-start.3
  3.9 0.7 copy-done.3
  4.6 74.6 %shard_map.46 = bf16[8,256,256]{2,1,0:T(8,128)(2,1)S(1)} custom-call(bf16[8,256,256]{2,1,0:T(8,128)(2,1)S(1)} %copy-done.1, f32[3,256]{1,0:T(4,128)S(1)} %copy-done.2, f32[3,256]{1,0:T(4,128)S(1)} %copy-done.3, bf16[3,3,768,256]{3,2,1,0:T(8,128)(2,1)S(1)} %bitcast.1), custom_call_target="tpu_custom_call" | custom-call | tf_op jit(solution)/shard_map/pallas_call | solution.py:406
  79.2 1.0 %copy.6 = bf16[8,256,256]{2,1,0:T(8,128)(2,1)} copy(bf16[8,256,256]{2,1,0:T(8,128)(2,1)S(1)} %shard_map.46) | data formatting | bytes 2097152
Async XLA Ops:
  0.0 2.0 %copy-start = (bf16[3,3,3,256,256]{4,3,2,1,0:T(8,128)(2,1)S(1)}, bf16[3,3,3,256,256]{4,3,2,1,0:T(8,128)(2,1)}, u32[]{:S(2)}) copy-start(bf16[3,3,3,256,256]{4,3,2,1,0:T(8,128)(2,1)} %param.7) | copy-start | bytes 10616836
  2.0 1.2 %copy-start.1 = (bf16[8,256,256]{2,1,0:T(8,128)(2,1)S(1)}, bf16[8,256,256]{2,1,0:T(8,128)(2,1)}, u32[]{:S(2)}) copy-start(bf16[8,256,256]{2,1,0:T(8,128)(2,1)} %x_hbm.1) | copy-start | bytes 3145732
  3.2 0.7 copy-start.2
  3.9 0.7 copy-start.3

commit v2 on v1

--- a/solution.py
+++ b/solution.py
@@ -61,8 +61,8 @@
 
 
 def streamed(
-    x_hbm, g_ref, b_ref, w_hbm, out_hbm,
-    xs, n0, taps, n1, m1, n2, x1, x2, y, w,
+    x_hbm, g_hbm, b_hbm, w_hbm, out_hbm,
+    xs, n0, taps, n1, m1, n2, x1, x2, y, w, g_ref, b_ref,
     load_sem, w_sem, dn_send, dn_recv, up_send, up_recv, side_send, side_recv,
     swap_send, swap_recv, rim_send, rim_recv, out_sem,
 ):
@@ -174,6 +174,10 @@
     def _(s):
         load(s).start()
 
+    load_g = pltpu.make_async_copy(g_hbm, g_ref, w_sem.at[3])
+    load_b = pltpu.make_async_copy(b_hbm, b_ref, w_sem.at[4])
+    load_g.start()
+    load_b.start()
     for layer in range(3):
         load_w(layer).start()
 
@@ -225,13 +229,25 @@
     def _():
         corner_up.start()
 
+    @pl.when(i == shift - 1)
+    def _():
+        @pl.loop(1, slots + 1)
+        def _(s):
+            halo_down(s).start()
+
+    @pl.when(i == shift)
+    def _():
+        @pl.loop(1, slots + 1)
+        def _(s):
+            halo_up(s).start()
+
     @pl.loop(1, slots + 1)
     def _(s):
-        @pl.when(has_below)
+        @pl.when(has_below & (i != shift - 1))
         def _():
             halo_down(s).start()
 
-        @pl.when(has_above)
+        @pl.when(has_above & (i != shift))
         def _():
             halo_up(s).start()
 
@@ -262,6 +278,8 @@
     def _():
         corner_up.wait_recv()
 
+    load_g.wait()
+    load_b.wait()
     load_w(0).wait()
 
     @pl.loop(0, slots + 2)
@@ -408,8 +426,8 @@
         out_shape=jax.ShapeDtypeStruct(context_map.shape, bf16),
         in_specs=[
             pl.BlockSpec(memory_space=pltpu.HBM),
-            pl.BlockSpec(memory_space=pltpu.VMEM),
-            pl.BlockSpec(memory_space=pltpu.VMEM),
+            pl.BlockSpec(memory_space=pltpu.HBM),
+            pl.BlockSpec(memory_space=pltpu.HBM),
             pl.BlockSpec(memory_space=pltpu.HBM),
         ],
         out_specs=pl.BlockSpec(memory_space=pltpu.HBM),
@@ -424,8 +442,10 @@
             pltpu.VMEM((slots, tile_rows * wide, channels), bf16),
             pltpu.VMEM((slots,) + cell, bf16),
             pltpu.VMEM((3, 3, 3 * channels, channels), bf16),
+            pltpu.VMEM((3, channels), jnp.float32),
+            pltpu.VMEM((3, channels), jnp.float32),
             dma((slots,)),
-            dma((3,)),
+            dma((5,)),
             dma((slots,)), dma((slots,)),
             dma((slots,)), dma((slots,)),
             dma((3,)), dma((3,)),
@@ -434,7 +454,7 @@
             dma((slots,)),
         ],
         compiler_params=pltpu.CompilerParams(
-            collective_id=0, has_side_effects=True, vmem_limit_bytes=48 * 1024 * 1024
+            collective_id=0, has_side_effects=True, vmem_limit_bytes=67043328
         ),
     )(
         context_map,

time: 80.4 us -> 76.8 us (0.955)
  local copies, waits for them, and re-layouts: 5.57 us -> 2.26 us
    unnamed x9 -> x1, local copies, waits for them, and re-layouts: 5.57 us -> 2.26 us
where the time goes in v2:
time: 76.8 us; the launch traced here: 76.6 us
  Pallas kernels  74.3 us (97%)
  local copies, waits for them, and re-layouts  2.26 us (3%)
    pallas_call x1, Pallas kernels, streamed_shards(): pl.pallas_call(streamed, out_shape=jax.ShapeDtypeStruct(context_map.shape...  74.3 us
    unnamed x1, local copies, waits for them, and re-layouts  2.26 us

profile of v2, /device:TPU:0, one launch (start us, length us, event | category | flops | bytes accessed | tf_op | source)
XLA Modules:
  0.0 76.6 jit_solution(9834099781141115160)
XLA Ops:
  0.0 74.3 %shard_map.46 = bf16[8,256,256]{2,1,0:T(8,128)(2,1)} custom-call(bf16[8,256,256]{2,1,0:T(8,128)(2,1)} %x_hbm.1, f32[3,256]{1,0:T(4,128)} %g_hbm.1, f32[3,256]{1,0:T(4,128)} %b_hbm.1, bf16[3,3,768,256]{3,2,1,0:T(8,128)(2,1)} %bitcast.1), custom_call_target="tpu_custom_call" | custom-call | tf_op jit(solution)/shard_map/pallas_call | solution.py:424
  74.3 2.3 %copy.6 = bf16[8,256,256]{2,1,0:T(8,128)(2,1)} copy(bf16[8,256,256]{2,1,0:T(8,128)(2,1)} %shard_map.46) | data formatting | bytes 2097152

commit v3 on v2

--- a/solution.py
+++ b/solution.py
@@ -61,10 +61,10 @@
 
 
 def streamed(
-    x_hbm, g_hbm, b_hbm, w_hbm, out_hbm,
-    xs, n0, taps, n1, m1, n2, x1, x2, y, w, g_ref, b_ref,
+    x_hbm, g_hbm, b_hbm, w_hbm, out_ref,
+    xs, n0, taps, n1, m1, n2, x1, x2, relayed, w, g_ref, b_ref,
     load_sem, w_sem, dn_send, dn_recv, up_send, up_recv, side_send, side_recv,
-    swap_send, swap_recv, rim_send, rim_recv, out_sem,
+    swap_send, swap_recv, rim_send, rim_recv, relay_send, relay_recv,
 ):
     tile_rows, tile_cols, channels = x_hbm.shape
     halo, wide = dilations[0], dilations[1]
@@ -144,10 +144,42 @@
         for s in (1, 2)
     ]
 
-    def store(s):
-        return pltpu.make_async_copy(
-            y.at[s - 1], out_hbm.at[:, columns(s), :], out_sem.at[s - 1]
-        )
+    before, after = shift - 2, shift + 1
+    near_middle = (i >= before) & (i <= after)
+    across = jnp.where(i < shift, lax.rem(i + 2, n), lax.rem(i + n - 2, n))
+
+    def relay_row(s):
+        return jnp.where(lax.rem(s, 2) == 1, before, after)
+
+    def relay_down(s):
+        return remote(
+            x_hbm.at[tile_rows - halo :, columns(s), :], relayed.at[0, s - 1],
+            dn_send.at[s - 1], relay_recv.at[0, s - 1], relay_row(s), c,
+        )
+
+    def relay_up(s):
+        return remote(
+            x_hbm.at[:halo, columns(s), :], relayed.at[1, s - 1],
+            up_send.at[s - 1], relay_recv.at[1, s - 1], relay_row(s), c,
+        )
+
+    def forward_down(s):
+        return remote(
+            relayed.at[0, s - 1], xs.at[s, :halo],
+            relay_send.at[0, s - 1], dn_recv.at[s - 1], shift, c,
+        )
+
+    def forward_up(s):
+        return remote(
+            relayed.at[1, s - 1], xs.at[s, halo + tile_rows :],
+            relay_send.at[1, s - 1], up_recv.at[s - 1], shift - 1, c,
+        )
+
+    def relay(s):
+        relay_down(s).wait_recv()
+        forward_down(s).start()
+        relay_up(s).wait_recv()
+        forward_up(s).start()
 
     def norm(values, layer):
         values = values.astype(jnp.float32)
@@ -212,12 +244,16 @@
         greet(below, c)
         greet(below, other)
 
+    @pl.when(near_middle)
+    def _():
+        greet(across, c)
+
     n0[slots + 1] = zeros(n0.shape[1:])
     n1[slots + 1] = zeros(n1.shape[1:])
     m1[slots + 1] = zeros(m1.shape[1:])
     n2[slots + 2] = zeros(n2.shape[1:])
     n2[slots + 3] = zeros(n2.shape[1:])
-    pl.semaphore_wait(barrier, 2 + 2 * jnp.minimum(i, 1) + 2 * jnp.minimum(n - 1 - i, 1))
+    pl.semaphore_wait(barrier, 2 + 2 * jnp.minimum(i, 1) + 2 * jnp.minimum(n - 1 - i, 1) + near_middle.astype(jnp.int32))
 
     side.start()
 
@@ -228,21 +264,17 @@
     @pl.when(has_above)
     def _():
         corner_up.start()
-
-    @pl.when(i == shift - 1)
-    def _():
-        @pl.loop(1, slots + 1)
-        def _(s):
-            halo_down(s).start()
-
-    @pl.when(i == shift)
-    def _():
-        @pl.loop(1, slots + 1)
-        def _(s):
-            halo_up(s).start()
 
     @pl.loop(1, slots + 1)
     def _(s):
+        @pl.when(i == shift - 1)
+        def _():
+            relay_down(s).start()
+
+        @pl.when(i == shift)
+        def _():
+            relay_up(s).start()
+
         @pl.when(has_below & (i != shift - 1))
         def _():
             halo_down(s).start()
@@ -284,6 +316,14 @@
 
     @pl.loop(0, slots + 2)
     def _(s):
+        @pl.when((i == before) & (s < slots // 2))
+        def _():
+            relay(2 * s + 1)
+
+        @pl.when((i == after) & (s < slots // 2))
+        def _():
+            relay(2 * s + 2)
+
         @pl.when((s > 0) & (s <= slots))
         def _():
             arrive(s)
@@ -365,8 +405,7 @@
             at = s - 2
             response = dot(row_of(n2, at + 1, 2 * outward), w[2, 1])
             current = residual(x2[at - 1].reshape(tile_rows, wide, channels), response, 2)
-            y[at - 1] = current.reshape(tile_rows, wide, channels)
-            store(at).start()
+            out_ref[:, columns(at), :] = current.reshape(tile_rows, wide, channels)
 
     side.wait_send()
     rim_own.wait_send()
@@ -393,7 +432,14 @@
             halo_up(s).wait_send()
 
         swap(s).wait_send()
-        store(s).wait()
+
+    @pl.loop(0, slots // 2)
+    def _(k):
+        for row, s in ((before, 2 * k + 1), (after, 2 * k + 2)):
+            @pl.when(i == row)
+            def _():
+                forward_down(s).wait_send()
+                forward_up(s).wait_send()
 
 
 def paired(mesh, shape):
@@ -406,6 +452,7 @@
         and dilations[2] == 2 * dilations[1]
         and dilations[1] % tile_rows == 0
         and mesh["row"] > 2
+        and tile_cols % (2 * dilations[1]) == 0
         and tile_rows == 2 * dilations[0]
         and tile_cols % dilations[1] == 0
         and tile_cols >= dilations[2]
@@ -430,7 +477,7 @@
             pl.BlockSpec(memory_space=pltpu.HBM),
             pl.BlockSpec(memory_space=pltpu.HBM),
         ],
-        out_specs=pl.BlockSpec(memory_space=pltpu.HBM),
+        out_specs=pl.BlockSpec(memory_space=pltpu.VMEM),
         scratch_shapes=[
             pltpu.VMEM((slots + 1, tall, wide, channels), bf16),
             pltpu.VMEM((slots + 2, tall, wide, channels), bf16),
@@ -440,7 +487,7 @@
             pltpu.VMEM((slots + 4,) + cell, bf16),
             pltpu.VMEM((slots, tile_rows * wide, channels), bf16),
             pltpu.VMEM((slots, tile_rows * wide, channels), bf16),
-            pltpu.VMEM((slots,) + cell, bf16),
+            pltpu.VMEM((2, slots, halo, wide, channels), bf16),
             pltpu.VMEM((3, 3, 3 * channels, channels), bf16),
             pltpu.VMEM((3, channels), jnp.float32),
             pltpu.VMEM((3, channels), jnp.float32),
@@ -451,7 +498,7 @@
             dma((3,)), dma((3,)),
             dma((slots,)), dma((slots,)),
             dma((4,)), dma((4,)),
-            dma((slots,)),
+            dma((2, slots)), dma((2, slots)),
         ],
         compiler_params=pltpu.CompilerParams(
             collective_id=0, has_side_effects=True, vmem_limit_bytes=67043328

time: 76.8 us -> 77.5 us (level)
  Pallas kernels: 74.3 us -> 75.1 us
    pallas_call x1, Pallas kernels: 74.3 us -> 75.1 us  [streamed_shards(): pl.pallas_call(streamed, out_shape=jax.ShapeDtypeStruct(context_map.shape...]
where the time goes in v3:
time: 77.5 us; the launch traced here: 77.4 us
  Pallas kernels  75.1 us (97%)
  local copies, waits for them, and re-layouts  2.26 us (3%)
    pallas_call x1, Pallas kernels, streamed_shards(): pl.pallas_call(streamed, out_shape=jax.ShapeDtypeStruct(context_map.shape...  75.1 us
    unnamed x1, local copies, waits for them, and re-layouts  2.26 us

profile of v3, /device:TPU:0, one launch (start us, length us, event | category | flops | bytes accessed | tf_op | source)
XLA Modules:
  0.0 77.4 jit_solution(13738662518762227521)
XLA Ops:
  0.0 75.1 %shard_map.46 = bf16[8,256,256]{2,1,0:T(8,128)(2,1)} custom-call(bf16[8,256,256]{2,1,0:T(8,128)(2,1)} %x_hbm.1, f32[3,256]{1,0:T(4,128)} %g_hbm.1, f32[3,256]{1,0:T(4,128)} %b_hbm.1, bf16[3,3,768,256]{3,2,1,0:T(8,128)(2,1)} %bitcast.1), custom_call_target="tpu_custom_call" | custom-call | tf_op jit(solution)/shard_map/pallas_call | solution.py:471
  75.1 2.3 %copy.6 = bf16[8,256,256]{2,1,0:T(8,128)(2,1)} copy(bf16[8,256,256]{2,1,0:T(8,128)(2,1)} %shard_map.46) | data formatting | bytes 2097152
